TPU v7x, 32 devices: a whole 2x2x4 slice. The times are simulated.
32 devices in a mesh: gx: 4 (over y, x), gy: 8 (over z, core).
Axes of the slice: x: 2, y: 2, z: 4, core: 2. Of those that a mesh axis runs over, the one named last changes fastest.
Arguments:
- inputs: bfloat16 [512, 8192], P('gx', 'gy'), may hold values from -6 to 6
- out_grad: bfloat16 [512, 8192], P('gx', 'gy'), may hold values from -1.1953125 to 1.1953125
- pre_act: bfloat16 [512, 32768], P('gy', 'gx'), may hold values from -6 to 6
- w_in: bfloat16 [8192, 32768], P('gy', 'gx'), may hold values from -0.0625 to 0.0625
- w_out: bfloat16 [32768, 8192], P('gx', 'gy'), may hold values from -0.03125 to 0.03125
- counts: int32 [4], replicated, may hold values from 1 to 128, 320 in all
Outputs:
- in_grad: bfloat16 [512, 8192], P('gx', 'gy')
- w_in_grad: bfloat16 [8192, 32768], P('gy', 'gx')
- w_out_grad: bfloat16 [32768, 8192], P('gx', 'gy')
Inputs may be any that keep to these rules, and one draw needn't show every extreme that they name: In batch shard s (token slots s * 128 to (s + 1) * 128 - 1) the first counts[s] slots are live and the rest are padding; the counts add up to exactly 320, and at least one shard is full.
All inputs are finite; a program needn't handle non-finite values.
Results may differ from a plain program's by a relative error of at most 0.0051.
Values may be sent and summed in bfloat16 or wider, within the bound.
No kernel may reach another device: no remote copies, remote signals or barrier semaphores. Data moves between devices by JAX's collectives and lax.ppermute only.
A program may use at most 192 MiB of HBM per device.

v0:
```python
import math
import jax
import jax.numpy as jnp
from jax import lax
from jax.sharding import PartitionSpec as P

gelu_scale = math.sqrt(2.0 / math.pi)
cubic_coef = 0.044715


def gelu_value(pre):
    tangent = jnp.tanh(gelu_scale * (pre + cubic_coef * pre * pre * pre))
    return 0.5 * pre * (1.0 + tangent)


def gelu_slope(pre):
    tangent = jnp.tanh(gelu_scale * (pre + cubic_coef * pre * pre * pre))
    return 0.5 * (1.0 + tangent) + 0.5 * pre * (1.0 - tangent * tangent) * gelu_scale * (
        1.0 + 3.0 * cubic_coef * pre * pre
    )


def token_sum(left, right):
    return lax.dot_general(
        left, right, (((0,), (0,)), ((), ())), preferred_element_type=jnp.float32
    )


def contract_last(left, right):
    return lax.dot_general(
        left, right, (((1,), (1,)), ((), ())), preferred_element_type=jnp.float32
    )


def live_mask(counts, shard_rows, all_rows, shards):
    positions = jnp.arange(all_rows, dtype=jnp.int32)
    owner_shard = positions // shard_rows
    one_hot = owner_shard[:, None] == jnp.arange(shards, dtype=jnp.int32)[None, :]
    own_count = jnp.sum(jnp.where(one_hot, counts[None, :], 0), axis=1)
    return positions % shard_rows < own_count


def packed_index(counts, shard_rows, shards, live_rows):
    ends = jnp.cumsum(counts)
    starts = ends - counts
    packed = jnp.arange(live_rows, dtype=jnp.int32)
    which = jnp.sum((ends[None, :] <= packed[:, None]).astype(jnp.int32), axis=1)
    one_hot = which[:, None] == jnp.arange(shards, dtype=jnp.int32)[None, :]
    begin = jnp.sum(jnp.where(one_hot, starts[None, :], 0), axis=1)
    return which * shard_rows + packed - begin


def body(inputs, out_grad, pre_act, w_in, w_out, counts):
    shard_rows = inputs.shape[0]
    shards = lax.axis_size("gx")
    all_rows = shard_rows * shards
    live_rows = all_rows * 5 // 8
    row_index = packed_index(counts, shard_rows, shards, live_rows)
    gathered_x, gathered_dy = (
        lax.all_gather(inputs, "gx", axis=0, tiled=True),
        lax.all_gather(out_grad, "gx", axis=0, tiled=True),
    )
    is_live = live_mask(counts, shard_rows, all_rows, shards)
    masked_grad = jnp.where(is_live[:, None], gathered_dy, jnp.zeros_like(gathered_dy))
    whole_pre = lax.all_gather(pre_act, "gy", axis=0, tiled=True).astype(jnp.float32)
    activation = gelu_value(whole_pre).astype(jnp.bfloat16)
    sent_grad = jnp.take(masked_grad, row_index, axis=0)
    sent_pre = jnp.take(whole_pre, row_index, axis=0)
    hidden_total = lax.psum(contract_last(sent_grad, w_out), "gy")
    sent_hidden = (hidden_total * gelu_slope(sent_pre)).astype(jnp.bfloat16)
    hidden_grad = (
        jnp.zeros((all_rows, sent_hidden.shape[1]), jnp.bfloat16).at[row_index].set(sent_hidden)
    )
    w_out_grad = token_sum(activation, masked_grad)
    w_in_grad = token_sum(gathered_x, hidden_grad)
    in_part = lax.psum_scatter(
        contract_last(hidden_grad, w_in), "gx", scatter_dimension=0, tiled=True
    )
    return (
        in_part.astype(jnp.bfloat16),
        w_in_grad.astype(jnp.bfloat16),
        w_out_grad.astype(jnp.bfloat16),
    )


def solution(mesh):
    return jax.shard_map(
        body,
        mesh=mesh,
        in_specs=(P("gx", "gy"), P("gx", "gy"), P("gy", "gx"), P("gy", "gx"), P("gx", "gy"), P()),
        out_specs=(P("gx", "gy"), P("gy", "gx"), P("gx", "gy")),
        check_vma=False,
    )
```

profile of v0, /device:TPU:0, one launch (start us, length us, event | category | flops | bytes accessed | tf_op | source)
XLA Modules:
  0.0 445.9 jit_solution(4498768962344689414)
XLA Ops:
  7.2 0.0 all-gather.4.cloned.1.call-start
  7.2 0.7 all-gather.4.cloned.1.call-update
  7.9 0.0 all-gather.6.cloned.1.call-start
  7.9 0.7 all-gather.6.cloned.1.call-update
  8.6 0.0 all-reduce.2.cloned.1.call-start
  8.7 0.8 reduce-window.8
  9.5 0.1 convert_reduce_fusion
  9.6 0.7 bitcast_subtract_fusion
  10.3 0.1 select_reduce_fusion.1
  10.4 0.7 select_reduce_fusion
  11.2 27.9 %all-gather.4.cloned.1.call-done = bf16[512,1024]{1,0:T(8,128)(2,1)} async-done(((bf16[128,1024]{1,0:T(8,128)(2,1)}), bf16[512,1024]{1,0:T(8,128)(2,1)}) %all-gather.4.cloned.1.call-update) | async-done | bytes 1048592 | tf_op jit(solution)/shard_map/all_gather | solution.py:61
  39.1 1.4 broadcast_select_fusion
  40.5 2.1 gather_fusion
  42.6 19.9 %fusion.20 = f32[320,8192]{1,0:T(8,128)} fusion(bf16[8192,1024]{1,0:T(8,128)(2,1)} %param.10, bf16[320,1024]{1,0:T(8,128)(2,1)S(1)} %gather_fusion, pred[320]{0:T(512)(128)(4,1)S(1)} %compare_and_fusion), kind=kOutput, calls=%fused_computation.28 | convolution fusion | flops 5369036800 | bytes 27918656 | tf_op jit(solution)/shard_map/dot_general | solution.py:30
  62.5 0.0 all-reduce.2.cloned.1.call-update
  62.5 0.0 all-gather.8.cloned.1.call-start
  62.6 0.5 all-gather.8.cloned.1.call-update
  63.1 0.3 reduce-scatter.2.cloned.1.call-start
  63.5 59.3 %all-gather.6.cloned.1.call-done = bf16[512,8192]{1,0:T(8,128)(2,1)} async-done(((bf16[64,8192]{1,0:T(8,128)(2,1)}), bf16[512,8192]{1,0:T(8,128)(2,1)}) %all-gather.6.cloned.1.call-update) | async-done | bytes 8388624 | tf_op jit(solution)/shard_map/all_gather | solution.py:65
  122.8 12.1 %convert_element_type.25 = f32[512,8192]{1,0:T(8,128)} convert(bf16[512,8192]{1,0:T(8,128)(2,1)} %all-gather.6.cloned.1.call-done) | non-fusion elementwise | flops 4194304 | bytes 25165824 | tf_op jit(solution)/shard_map/convert_element_type | solution.py:65
  134.9 19.9 %gather_fusion.1 = f32[320,8192]{1,0:T(8,128)} fusion(f32[512,8192]{1,0:T(8,128)} %convert_element_type.25, s32[1024]{0:T(1024)S(1)} %pad_clamp_fusion), kind=kCustom, calls=%fused_computation.1 | custom fusion | bytes 20972800 | tf_op jit(solution)/shard_map/jit(_take)/gather | solution.py:68
  154.8 184.5 %all-reduce.2.cloned.1.call-done = f32[320,8192]{1,0:T(8,128)} async-done(((f32[320,8192]{1,0:T(8,128)}), f32[320,8192]{1,0:T(8,128)}) %all-reduce.2.cloned.1.call-update) | async-done | bytes 10485776 | tf_op jit(solution)/shard_map/psum | solution.py:69
  339.3 12.5 %fusion.11 = bf16[320,8192]{1,0:T(8,128)(2,1)} fusion(f32[320,8192]{1,0:T(8,128)} %all-reduce.2.cloned.1.call-done, f32[320,8192]{1,0:T(8,128)} %gather_fusion.1, pred[320]{0:T(512)(128)(4,1)S(1)} %compare_and_fusion), kind=kLoop, calls=%fused_computation.19 | loop fusion | flops 52428800 | bytes 26214720 | tf_op jit(solution)/shard_map/convert_element_type | solution.py:70
  351.8 14.5 %scatter_custom_fusion = bf16[512,8192]{1,0:T(8,128)(2,1)} fusion(s32[320]{0:T(512)S(1)} %fusion.30, bf16[320,8192]{1,0:T(8,128)(2,1)} %fusion.11, bf16[]{:T(256)} %constant.45.clone.1), kind=kCustom, calls=%fused_computation.25 | custom fusion | bytes 8389120 | tf_op jit(solution)/shard_map/scatter | solution.py:72
  366.3 16.0 %fusion.36 = f32[512,1024]{1,0:T(8,128)} fusion(bf16[512,8192]{1,0:T(8,128)(2,1)} %scatter_custom_fusion, bf16[1024,8192]{1,0:T(8,128)(2,1)} %param.9), kind=kOutput, calls=%fused_computation.61 | convolution fusion | flops 8589934592 | bytes 27262976 | tf_op jit(solution)/shard_map/dot_general | solution.py:30
  382.3 0.0 reduce-scatter.2.cloned.1.call-update
  382.3 0.0 all-gather.8.cloned.1.call-done
  382.4 15.1 %convert_bitcast_fusion = bf16[1024,8192]{0,1:T(8,128)(2,1)} fusion(bf16[512,8192]{1,0:T(8,128)(2,1)} %scatter_custom_fusion, bf16[512,1024]{1,0:T(8,128)(2,1)} %all-gather.8.cloned.1.call-done), kind=kOutput, calls=%fused_computation.9 | convolution fusion | flops 8598323200 | bytes 26214400 | tf_op jit(solution)/shard_map/dot_general | solution.py:24
  397.4 21.3 %copy.11 = bf16[1024,8192]{1,0:T(8,128)(2,1)} copy(bf16[1024,8192]{0,1:T(8,128)(2,1)} %convert_bitcast_fusion) | data formatting | bytes 33554432
  418.7 18.7 %convolution_convert_fusion = bf16[8192,1024]{1,0:T(8,128)(2,1)} fusion(bf16[512,1024]{1,0:T(8,128)(2,1)S(1)} %broadcast_select_fusion, bf16[512,8192]{1,0:T(8,128)(2,1)} %all-gather.6.cloned.1.call-done), kind=kOutput, calls=%fused_computation.12 | convolution fusion | flops 8640266240 | bytes 26214400 | tf_op jit(solution)/shard_map/dot_general | solution.py:24
  437.4 0.0 reduce-scatter.2.cloned.1.call-done
  437.4 1.8 convert_element_type.27
  (6 shorter events, 0.1 us)
Async XLA Ops:
  7.2 31.9 %all-gather.4.cloned.1.call-start = ((), (), s32[]{:S(2)}) async-start(), calls=%async_computation.1 | async-start | bytes 1310720 | tf_op jit(solution)/shard_map/all_gather | solution.py:61
  7.9 114.9 %all-gather.6.cloned.1.call-start = ((), (), s32[]{:S(2)}) async-start(), calls=%async_computation.3 | async-start | bytes 9437184 | tf_op jit(solution)/shard_map/all_gather | solution.py:65
  8.6 330.6 %all-reduce.2.cloned.1.call-start = ((), (), s32[]{:S(2)}) async-start(), calls=%async_computation.2 | async-start | bytes 20971520 | tf_op jit(solution)/shard_map/psum | solution.py:69
  62.5 319.8 %all-gather.8.cloned.1.call-start = ((), (), s32[]{:S(2)}) async-start(), calls=%async_computation.5 | async-start | bytes 1310720 | tf_op jit(solution)/shard_map/all_gather | solution.py:60
  63.1 374.3 %reduce-scatter.2.cloned.1.call-start = ((), (), s32[]{:S(2)}) async-start(), calls=%async_computation.4 | async-start | bytes 2621440 | tf_op jit(solution)/shard_map/reduce_scatter | solution.py:76
Sparse Core Ops, SparseCore 0:
  9.8 29.2 all-gather.3
  40.7 82.0 all-gather.5
  125.7 213.5 all-reduce.1
  341.0 26.6 all-gather.7
  382.4 35.3 reduce-scatter.1
where the time goes:
time: 451 us; the launch traced here: 446 us
  waiting for transfers between devices  274 us (61%)
  matrix products  69.7 us (15%)
  local copies, waits for them, and re-layouts  57.8 us (13%)
  other arithmetic  30.2 us (7%)
  between operations  14.1 us (3%)
    psum x1, waiting for transfers between devices, body(): hidden_total = lax.psum(contract_last(sent_grad, w_out), 'gy')  185 us
    all_gather x1, waiting for transfers between devices, body(): lax.all_gather(pre_act, 'gy', axis=0, tiled=True).astype(jnp.float32)  59.3 us
    dot_general x2, matrix products, contract_last(): lax.dot_general(left, right, (((1,), (1,)), ((), ())), preferred_element_...  35.9 us
    dot_general x2, matrix products, token_sum(): lax.dot_general(left, right, (((0,), (0,)), ((), ())), preferred_element_...  33.7 us
    all_gather x1, waiting for transfers between devices, body(): lax.all_gather(out_grad, 'gx', axis=0, tiled=True)  27.9 us
    unnamed x1, local copies, waits for them, and re-layouts  21.3 us
    gather x1, local copies, waits for them, and re-layouts, body(): sent_pre = jnp.take(whole_pre, row_index, axis=0)  19.9 us
    scatter x1, local copies, waits for them, and re-layouts, body(): jnp.zeros((all_rows, sent_hidden.shape[1]), jnp.bfloat16).at[row_index]  14.5 us
  transfers between devices with their start and end apart: 5, of which 3 were waited for; matrix products, arithmetic and copies ran while one was open for 35% of the time, Pallas kernels for 0%

commit v1 on v0

--- a/solution.py
+++ b/solution.py
@@ -66,7 +66,7 @@
     activation = gelu_value(whole_pre).astype(jnp.bfloat16)
     sent_grad = jnp.take(masked_grad, row_index, axis=0)
     sent_pre = jnp.take(whole_pre, row_index, axis=0)
-    hidden_total = lax.psum(contract_last(sent_grad, w_out), "gy")
+    hidden_total = jnp.sum(lax.all_gather(contract_last(sent_grad, w_out), "gy"), axis=0)
     sent_hidden = (hidden_total * gelu_slope(sent_pre)).astype(jnp.bfloat16)
     hidden_grad = (
         jnp.zeros((all_rows, sent_hidden.shape[1]), jnp.bfloat16).at[row_index].set(sent_hidden)

time: 451 us -> 969 us (2.15)
  waiting for transfers between devices: 274 us -> 753 us
  other arithmetic: 30.2 us -> 64.9 us
    all_gather x0 -> x1, waiting for transfers between devices: none -> 663 us  [body(): lax.all_gather(contract_last(sent_grad, w_out), 'gy')]
    psum x1 -> x0, waiting for transfers between devices: 185 us -> none  [body(): hidden_total = lax.psum(contract_last(sent_grad, w_out), 'gy')]
    reduce_sum x0 -> x1, other arithmetic: none -> 30.6 us  [body(): jnp.sum(lax.all_gather(contract_last(sent_grad, w_out), 'gy'), axis=0)]
  transfers between devices with their start and end apart: 5 -> 5, of which waited for: 3 -> 3; matrix products, arithmetic and copies ran while one was open for 35% -> 20% of each run, Pallas kernels for 0% -> 0%
where the time goes in v1:
time: 969 us; the launch traced here: 963 us
  waiting for transfers between devices  753 us (78%)
  matrix products  69.6 us (7%)
  other arithmetic  64.9 us (7%)
  local copies, waits for them, and re-layouts  61.5 us (6%)
  between operations  14.1 us (1%)
    all_gather x1, waiting for transfers between devices, body(): lax.all_gather(contract_last(sent_grad, w_out), 'gy')  663 us
    all_gather x1, waiting for transfers between devices, body(): lax.all_gather(pre_act, 'gy', axis=0, tiled=True).astype(jnp.float32)  59.6 us
    dot_general x2, matrix products, contract_last(): lax.dot_general(left, right, (((1,), (1,)), ((), ())), preferred_element_...  36 us
    dot_general x2, matrix products, token_sum(): lax.dot_general(left, right, (((0,), (0,)), ((), ())), preferred_element_...  33.6 us
    reduce_sum x1, other arithmetic, body(): jnp.sum(lax.all_gather(contract_last(sent_grad, w_out), 'gy'), axis=0)  30.6 us
    all_gather x1, waiting for transfers between devices, body(): lax.all_gather(out_grad, 'gx', axis=0, tiled=True)  27.9 us
    gather x1, local copies, waits for them, and re-layouts, body(): sent_pre = jnp.take(whole_pre, row_index, axis=0)  24 us
    unnamed x1, local copies, waits for them, and re-layouts  21.2 us
  transfers between devices with their start and end apart: 5, of which 3 were waited for; matrix products, arithmetic and copies ran while one was open for 20% of the time, Pallas kernels for 0%

profile of v1, /device:TPU:0, one launch (start us, length us, event | category | flops | bytes accessed | tf_op | source)
XLA Modules:
  0.0 963.1 jit_solution(4625633025669767278)
XLA Ops:
  7.2 0.0 all-gather.6.cloned.1.call-start
  7.2 0.7 all-gather.6.cloned.1.call-update
  7.9 0.0 all-gather.8.cloned.1.call-start
  7.9 0.7 all-gather.8.cloned.1.call-update
  8.6 0.0 all-gather.12.cloned.1.call-start
  8.7 0.8 reduce-window.8
  9.5 0.1 convert_reduce_fusion
  9.6 0.7 bitcast_subtract_fusion
  10.3 0.1 select_reduce_fusion.1
  10.4 0.7 select_reduce_fusion
  11.2 27.9 %all-gather.6.cloned.1.call-done = bf16[512,1024]{1,0:T(8,128)(2,1)} async-done(((bf16[128,1024]{1,0:T(8,128)(2,1)}), bf16[512,1024]{1,0:T(8,128)(2,1)}) %all-gather.6.cloned.1.call-update) | async-done | bytes 1048592 | tf_op jit(solution)/shard_map/all_gather | solution.py:61
  39.1 1.4 broadcast_select_fusion
  40.5 2.1 gather_fusion
  42.6 19.9 %fusion.20 = f32[320,8192]{1,0:T(8,128)} fusion(bf16[8192,1024]{1,0:T(8,128)(2,1)} %param.10, bf16[320,1024]{1,0:T(8,128)(2,1)S(1)} %gather_fusion, pred[320]{0:T(512)(128)(4,1)S(1)} %compare_and_fusion), kind=kOutput, calls=%fused_computation.28 | convolution fusion | flops 5369036800 | bytes 27918656 | tf_op jit(solution)/shard_map/dot_general | solution.py:30
  62.5 0.0 all-gather.12.cloned.1.call-update
  62.5 0.0 all-gather.10.cloned.1.call-start
  62.6 0.5 all-gather.10.cloned.1.call-update
  63.1 0.0 reduce-scatter.2.cloned.1.call-start
  63.2 59.6 %all-gather.8.cloned.1.call-done = bf16[512,8192]{1,0:T(8,128)(2,1)} async-done(((bf16[64,8192]{1,0:T(8,128)(2,1)}), bf16[512,8192]{1,0:T(8,128)(2,1)}) %all-gather.8.cloned.1.call-update) | async-done | bytes 8388624 | tf_op jit(solution)/shard_map/all_gather | solution.py:65
  122.8 16.1 %convert_element_type.25 = f32[512,8192]{1,0:T(8,128)} convert(bf16[512,8192]{1,0:T(8,128)(2,1)} %all-gather.8.cloned.1.call-done) | non-fusion elementwise | flops 4194304 | bytes 25165824 | tf_op jit(solution)/shard_map/convert_element_type | solution.py:65
  138.9 24.0 %gather_fusion.1 = f32[320,8192]{1,0:T(8,128)} fusion(f32[512,8192]{1,0:T(8,128)} %convert_element_type.25, s32[1024]{0:T(1024)S(1)} %pad_clamp_fusion), kind=kCustom, calls=%fused_computation.1 | custom fusion | bytes 20972800 | tf_op jit(solution)/shard_map/jit(_take)/gather | solution.py:68
  162.9 663.4 %all-gather.12.cloned.1.call-done = f32[2560,8192]{1,0:T(8,128)} async-done(((f32[320,8192]{1,0:T(8,128)}), f32[2560,8192]{1,0:T(8,128)}) %all-gather.12.cloned.1.call-update) | async-done | bytes 83886096 | tf_op jit(solution)/shard_map/all_gather | solution.py:69
  826.3 30.6 %reduce_sum.42 = f32[320,8192]{1,0:T(8,128)} reduce(f32[8,320,8192]{2,1,0:T(8,128)} %bitcast.2, f32[]{:T(128)} %constant.78.clone.1), dimensions={0}, to_apply=%region_4.5 | reduce | flops 18350080 | bytes 94371840 | tf_op jit(solution)/shard_map/reduce_sum | solution.py:69
  856.9 12.5 %fusion.11 = bf16[320,8192]{1,0:T(8,128)(2,1)} fusion(f32[320,8192]{1,0:T(8,128)} %reduce_sum.42, f32[320,8192]{1,0:T(8,128)} %gather_fusion.1, pred[320]{0:T(512)(128)(4,1)S(1)} %compare_and_fusion), kind=kLoop, calls=%fused_computation.19 | loop fusion | flops 52428800 | bytes 26214720 | tf_op jit(solution)/shard_map/convert_element_type | solution.py:70
  869.4 14.2 %scatter_custom_fusion = bf16[512,8192]{1,0:T(8,128)(2,1)} fusion(s32[320]{0:T(512)S(1)} %fusion.30, bf16[320,8192]{1,0:T(8,128)(2,1)} %fusion.11, bf16[]{:T(256)} %constant.45.clone.1), kind=kCustom, calls=%fused_computation.25 | custom fusion | bytes 8389120 | tf_op jit(solution)/shard_map/scatter | solution.py:72
  883.6 16.0 %fusion.36 = f32[512,1024]{1,0:T(8,128)} fusion(bf16[512,8192]{1,0:T(8,128)(2,1)} %scatter_custom_fusion, bf16[1024,8192]{1,0:T(8,128)(2,1)} %param.9), kind=kOutput, calls=%fused_computation.61 | convolution fusion | flops 8589934592 | bytes 27262976 | tf_op jit(solution)/shard_map/dot_general | solution.py:30
  899.6 0.0 reduce-scatter.2.cloned.1.call-update
  899.7 18.5 %convolution_convert_fusion = bf16[8192,1024]{1,0:T(8,128)(2,1)} fusion(bf16[512,1024]{1,0:T(8,128)(2,1)S(1)} %broadcast_select_fusion, bf16[512,8192]{1,0:T(8,128)(2,1)} %all-gather.8.cloned.1.call-done), kind=kOutput, calls=%fused_computation.12 | convolution fusion | flops 8640266240 | bytes 26214400 | tf_op jit(solution)/shard_map/dot_general | solution.py:24
  918.2 0.0 all-gather.10.cloned.1.call-done
  918.2 15.1 %convert_bitcast_fusion = bf16[1024,8192]{0,1:T(8,128)(2,1)} fusion(bf16[512,8192]{1,0:T(8,128)(2,1)} %scatter_custom_fusion, bf16[512,1024]{1,0:T(8,128)(2,1)} %all-gather.10.cloned.1.call-done), kind=kOutput, calls=%fused_computation.9 | convolution fusion | flops 8598323200 | bytes 26214400 | tf_op jit(solution)/shard_map/dot_general | solution.py:24
  933.3 21.2 %copy.11 = bf16[1024,8192]{1,0:T(8,128)(2,1)} copy(bf16[1024,8192]{0,1:T(8,128)(2,1)} %convert_bitcast_fusion) | data formatting | bytes 33554432
  954.5 0.0 reduce-scatter.2.cloned.1.call-done
  954.5 1.8 convert_element_type.27
  (6 shorter events, 0.1 us)
Async XLA Ops:
  7.2 31.9 %all-gather.6.cloned.1.call-start = ((), (), s32[]{:S(2)}) async-start(), calls=%async_computation.1 | async-start | bytes 1310720 | tf_op jit(solution)/shard_map/all_gather | solution.py:61
  7.9 114.9 %all-gather.8.cloned.1.call-start = ((), (), s32[]{:S(2)}) async-start(), calls=%async_computation.2 | async-start | bytes 9437184 | tf_op jit(solution)/shard_map/all_gather | solution.py:65
  8.6 817.6 %all-gather.12.cloned.1.call-start = ((), (), s32[]{:S(2)}) async-start(), calls=%async_computation.5 | async-start | bytes 94371840 | tf_op jit(solution)/shard_map/all_gather | solution.py:69
  62.5 855.6 %all-gather.10.cloned.1.call-start = ((), (), s32[]{:S(2)}) async-start(), calls=%async_computation.4 | async-start | bytes 1310720 | tf_op jit(solution)/shard_map/all_gather | solution.py:60
  63.1 891.4 %reduce-scatter.2.cloned.1.call-start = ((), (), s32[]{:S(2)}) async-start(), calls=%async_computation.3 | async-start | bytes 2621440 | tf_op jit(solution)/shard_map/reduce_scatter | solution.py:76
Sparse Core Ops, SparseCore 0:
  9.8 29.2 all-gather.5
  40.7 82.0 all-gather.7
  125.0 701.2 all-gather.11
  828.0 24.6 all-gather.9
  899.8 33.3 reduce-scatter.1
